TPU v7x, 32 devices: a whole 2x2x4 slice. The times are simulated.
32 devices in a mesh: tile: 2 (over y), strip: 4 (over x, core), focus: 4 (over z).
Axes of the slice: x: 2, y: 2, z: 4, core: 2. Of those that a mesh axis runs over, the one named last changes fastest.
Arguments:
- phi: float32 [512, 2048], P(('tile', 'strip')), parts along dimension 0, may hold values from -6 to 6
- target: int32 [512, 2048], P(('tile', 'strip')), parts along dimension 0, may hold values 0 or 1
- defocus_ids: int32 [8], P(('tile', 'focus')), parts along dimension 0, may hold values from 0 to 30
- kernels: float32 [2, 4, 48, 512], replicated, may hold values from -16 to 16
- psi: float32 [48, 512], replicated, may hold values from -3.140625 to 3.140625
- row_freqs: int32 [48], replicated, may hold values from -96 to 95, as said below
- col_freqs: int32 [512], replicated, may hold values from -1024 to 1023, as said below
Outputs:
- phi_next: float32 [512, 2048], P(('tile', 'strip')), parts along dimension 0
There are 2 independent parts, one for each index of `tile`. A program takes and returns all parts, laid end to end along the dimension named above; an argument that names none is the same for every part. Nothing has to cross between parts.
Inputs may be any that keep to these rules, and one draw needn't show every extreme that they name: `row_freqs`: distinct whole frequencies; the lowest and highest of the range are always among them. `col_freqs`: distinct whole frequencies; the lowest and highest of the range are always among them.
All inputs are finite; a program needn't handle non-finite values. No bound on the sum of `target` on one device may be relied on, other than what follows from the above.
Results may differ from a plain program's by a relative error of at most 0.02.
Values may be sent and summed in bfloat16 or wider, within the bound.
No kernel may reach another device: no remote copies, remote signals or barrier semaphores. Data moves between devices by JAX's collectives and lax.ppermute only.
A program may use at most 64 MiB of HBM per device.

v0:
```python
import jax
import jax.numpy as jnp
from jax import lax
from jax.sharding import PartitionSpec as P

MARGIN = 64
LEVELS = 31
SWEEPS = 2
slope_resist = 4.0
level_resist = 0.5
step_size = 1.0
flow_rate = 0.2


def padded_2(block, sides, width):
    for axis, dim in sides:
        count = lax.axis_size(axis)
        forward = [(i, i + 1) for i in range(count - 1)]
        backward = [(target, source) for source, target in forward]
        low = lax.ppermute(
            lax.slice_in_dim(block, block.shape[dim] - width, None, axis=dim), axis, forward
        )
        high = lax.ppermute(lax.slice_in_dim(block, 0, width, axis=dim), axis, backward)
        block = jnp.concatenate([low, block, high], axis=dim)
    return block


def tables(freq_list, period, length):
    positions = jnp.arange(length, dtype=jnp.int32)
    phase_int = jnp.mod(freq_list[:, None] * positions[None, :], period)
    angles = phase_int.astype(jnp.float32) * (2.0 * jnp.pi / period)
    return (jnp.cos(angles).astype(jnp.bfloat16), jnp.sin(angles).astype(jnp.bfloat16))


def product(lhs_mat, rhs_mat):
    return jnp.dot(lhs_mat, rhs_mat, preferred_element_type=jnp.float32)


def product_t(lhs_mat, rhs_mat):
    return lax.dot_general(
        lhs_mat, rhs_mat, (((1,), (1,)), ((), ())), preferred_element_type=jnp.float32
    )


def exact_t(lhs_mat, rhs_mat):
    return lax.dot_general(
        lhs_mat.astype(jnp.float32),
        rhs_mat,
        (((0,), (0,)), ((), ())),
        precision=lax.Precision.HIGHEST,
        preferred_element_type=jnp.float32,
    )


def spectral_rows(cos_part, sin_part, y_re, y_im):
    z_re = exact_t(cos_part, y_re) - exact_t(sin_part, y_im)
    z_im = exact_t(cos_part, y_im) + exact_t(sin_part, y_re)
    return jnp.concatenate([z_re, z_im], axis=1).astype(jnp.bfloat16)


def curvature_step(extended):
    padded = jnp.pad(extended, ((0, 0), (1, 1)))
    center = padded[1:-1, 1:-1]
    upper_row = padded[2:, 1:-1]
    lower_row = padded[:-2, 1:-1]
    right_col = padded[1:-1, 2:]
    left_col = padded[1:-1, :-2]
    diagonal = padded[2:, 2:] - padded[2:, :-2] - padded[:-2, 2:] + padded[:-2, :-2]
    grad_x = 0.5 * (upper_row - lower_row)
    grad_y = 0.5 * (right_col - left_col)
    second_x = upper_row - 2.0 * center + lower_row
    second_y = right_col - 2.0 * center + left_col
    cross_term = 0.25 * diagonal
    flow_term = (
        second_x * grad_y * grad_y - 2.0 * grad_x * grad_y * cross_term + second_y * grad_x * grad_x
    ) / (1.0 + grad_x * grad_x + grad_y * grad_y)
    return center + flow_rate * flow_term


def on_device(phi, target, defocus_ids, kernels, psi, row_freqs, col_freqs):
    strip_rows, col_count = phi.shape
    spectrum = psi.shape[1]
    kernel_count = kernels.shape[1]
    window_rows = strip_rows + 2 * MARGIN
    scale_norm = 1.0 / jnp.sqrt(jnp.float32(window_rows * col_count))
    row_cos, row_sin = tables(row_freqs, window_rows, window_rows)
    col_cos, col_sin = tables(col_freqs, col_count, col_count)
    forward = jnp.concatenate([col_cos, -col_sin], axis=0)
    adjoint = jnp.concatenate([col_sin, col_cos], axis=0)
    inner_cos = row_cos[:, MARGIN : MARGIN + strip_rows]
    inner_sin = row_sin[:, MARGIN : MARGIN + strip_rows]
    mask_bf = jnp.tanh(phi).astype(jnp.bfloat16)
    window = padded_2(mask_bf, (("strip", 0),), MARGIN)
    spec_pair = product_t(window, forward).astype(jnp.bfloat16)
    cos_half = product(row_cos, spec_pair)
    sin_half = product(row_sin, spec_pair)
    s_re = scale_norm * (cos_half[:, :spectrum] + sin_half[:, spectrum:])
    s_im = scale_norm * (cos_half[:, spectrum:] - sin_half[:, :spectrum])
    middle = (LEVELS - 1) / 2.0
    defocus = (defocus_ids[0].astype(jnp.float32) - middle) / middle
    phase_turn = defocus * psi
    cos_turn = jnp.cos(phase_turn)
    sin_turn = jnp.sin(phase_turn)
    k_re = kernels[0] * cos_turn - kernels[1] * sin_turn
    k_im = kernels[0] * sin_turn + kernels[1] * cos_turn
    g_pair = jnp.concatenate([k_re * s_re - k_im * s_im, k_re * s_im + k_im * s_re], axis=2).astype(
        jnp.bfloat16
    )
    head_part = jnp.einsum("fr,kfc->krc", inner_cos, g_pair, preferred_element_type=jnp.float32)
    tail_part = jnp.einsum("fr,kfc->krc", inner_sin, g_pair, preferred_element_type=jnp.float32)
    q_re = head_part[..., :spectrum] - tail_part[..., spectrum:]
    q_im = head_part[..., spectrum:] + tail_part[..., :spectrum]
    q_pair = (
        jnp.concatenate([q_re, q_im], axis=2)
        .astype(jnp.bfloat16)
        .reshape(kernel_count * strip_rows, 2 * spectrum)
    )
    e_re = (scale_norm * product(q_pair, forward)).reshape(kernel_count, strip_rows, col_count)
    e_im = (scale_norm * product(q_pair, adjoint)).reshape(kernel_count, strip_rows, col_count)
    intensity = jnp.mean(e_re * e_re + e_im * e_im, axis=0)
    resist = jax.nn.sigmoid(slope_resist * (intensity - level_resist))
    weight = (
        4.0
        * slope_resist
        / kernel_count
        * (resist - target.astype(jnp.float32))
        * resist
        * (1.0 - resist)
    )
    v_re = (weight * e_re).astype(jnp.bfloat16).reshape(kernel_count * strip_rows, col_count)
    v_im = (weight * e_im).astype(jnp.bfloat16).reshape(kernel_count * strip_rows, col_count)
    u_pair = (
        (product_t(v_re, forward) + product_t(v_im, adjoint))
        .astype(jnp.bfloat16)
        .reshape(kernel_count, strip_rows, 2 * spectrum)
    )
    head_back = jnp.einsum("fr,krc->kfc", inner_cos, u_pair, preferred_element_type=jnp.float32)
    tail_back = jnp.einsum("fr,krc->kfc", inner_sin, u_pair, preferred_element_type=jnp.float32)
    w_re = scale_norm * (head_back[..., :spectrum] + tail_back[..., spectrum:])
    w_im = scale_norm * (head_back[..., spectrum:] - tail_back[..., :spectrum])
    y_re = jnp.sum(k_re * w_re + k_im * w_im, axis=0)
    y_im = jnp.sum(k_re * w_im - k_im * w_re, axis=0)
    y_re, y_im = (
        lax.psum(y_re.astype(jnp.bfloat16), "focus").astype(jnp.float32),
        lax.psum(y_im.astype(jnp.bfloat16), "focus").astype(jnp.float32),
    )
    stacked = jnp.stack([y_re, y_im])[None]
    beside_all = padded_2(stacked.astype(jnp.bfloat16), (("strip", 0),), 1).astype(stacked.dtype)
    own_rows = spectral_rows(inner_cos, inner_sin, y_re, y_im)
    prev_rows = spectral_rows(
        row_cos[:, MARGIN + strip_rows :],
        row_sin[:, MARGIN + strip_rows :],
        beside_all[0, 0],
        beside_all[0, 1],
    )
    next_rows = spectral_rows(
        row_cos[:, :MARGIN], row_sin[:, :MARGIN], beside_all[2, 0], beside_all[2, 1]
    )
    grad_rows = scale_norm * product(
        jnp.concatenate([own_rows, prev_rows, next_rows], axis=0), forward
    )
    folded = grad_rows[:strip_rows]
    folded = (
        folded.at[:MARGIN]
        .add(grad_rows[strip_rows : strip_rows + MARGIN])
        .at[strip_rows - MARGIN :]
        .add(grad_rows[strip_rows + MARGIN :])
    )
    mask_slope = 1.0 - jnp.tanh(phi) * jnp.tanh(phi)
    level_set = phi - step_size * mask_slope * folded
    for counter in range(SWEEPS):
        extended_set = padded_2(level_set.astype(jnp.bfloat16), (("strip", 0),), 1).astype(
            level_set.dtype
        )
        level_set = curvature_step(extended_set)
    return level_set


def solution(mesh):
    return jax.shard_map(
        on_device,
        mesh=mesh,
        in_specs=(
            P(("tile", "strip"), None),
            P(("tile", "strip"), None),
            P(("tile", "focus")),
            P(),
            P(),
            P(),
            P(),
        ),
        out_specs=P(("tile", "strip"), None),
        check_vma=False,
    )
```

profile of v0, /device:TPU:1, one launch (start us, length us, event | category | flops | bytes accessed | tf_op | source)
XLA Modules:
  0.0 142.4 jit_solution(1823749973720386125)
XLA Ops:
  6.5 1.1 tanh_convert_fusion
  7.7 0.0 copy-start.9
  7.7 1.9 %collective-permute-start.1 = (bf16[64,2048]{1,0:T(8,128)(2,1)S(1)}, bf16[64,2048]{1,0:T(8,128)(2,1)S(1)}, u32[]{:S(2)}, u32[]{:S(2)}) collective-permute-start(bf16[64,2048]{1,0:T(8,128)(2,1)S(1)} %tanh_convert_fusion), channel_id=1, source_target_pairs={{4,0},{8,4},{12,8},{5,1},{9,5},{13,9},{6,2},{10,6},{14,10},{7,3},{... | collective-permute-start | bytes 786440 | tf_op jit(solution)/shard_map/ppermute | solution.py:23
  9.6 4.5 %collective-permute-start = (bf16[64,2048]{1,0:T(8,128)(2,1)S(1)}, bf16[64,2048]{1,0:T(8,128)(2,1)S(1)}, u32[]{:S(2)}, u32[]{:S(2)}) collective-permute-start(bf16[64,2048]{1,0:T(8,128)(2,1)S(1)} %tanh_convert_fusion), channel_id=1, source_target_pairs={{0,4},{4,8},{8,12},{1,5},{5,9},{9,13},{2,6},{6,10},{10,14},{3,7},{... | collective-permute-start | bytes 786440 | tf_op jit(solution)/shard_map/ppermute | solution.py:20
  14.1 18.9 %sine_convert_fusion = (bf16[512,2048]{1,0:T(8,128)(2,1)S(1)}, bf16[512,2048]{1,0:T(8,128)(2,1)S(1)}) fusion(s32[512]{0:T(512)} %param.21), kind=kLoop, calls=%fused_computation.8 | loop fusion | flops 16777216 | bytes 4196352 | tf_op jit(solution)/shard_map/convert_element_type | solution.py:32
  33.0 0.0 copy-start.10
  33.0 16.9 %fusion.22 = bf16[512,2048]{1,0:T(8,128)(2,1)S(1)} fusion(s32[512]{0:T(512)S(1)} %copy-done.9), kind=kLoop, calls=%fused_computation.50 | loop fusion | flops 18874368 | bytes 2099200 | tf_op jit(solution)/shard_map/neg | solution.py:88
  50.6 0.3 cosine_convert_fusion.1
  50.9 0.0 collective-permute-done.1
  50.9 0.0 collective-permute-done
  50.9 0.0 copy-start.8
  50.9 1.5 %convolution_convert_fusion = bf16[192,1024]{1,0:T(8,128)(2,1)S(1)} fusion(bf16[64,2048]{1,0:T(8,128)(2,1)S(1)} %collective-permute-done.1, bf16[64,2048]{1,0:T(8,128)(2,1)S(1)} %tanh_convert_fusion, bf16[64,2048]{1,0:T(8,128)(2,1)S(1)} %collective-permute-done, bf16[512,2048]{1,0:T(8,128)(2,1)S(1)} %fusion.22, bf16[512,2048]{1,0:T(8,128)(2,1)S(1)} %get-tuple-element.65), kind=kOutput, calls=%fused_computation.28 | convolution fusion | flops 816250880 | bytes 5373952 | tf_op jit(solution)/shard_map/dot_general | solution.py:40
  52.5 0.0 copy-start.7
  52.5 0.4 fusion.93
  52.9 0.4 fusion.92
  53.3 0.4 fusion.60
  53.7 0.2 subtract_convert_fusion
  53.9 0.1 add_convert_fusion.1
  54.0 0.4 convolution_bitcast_fusion
  54.4 0.4 convolution_bitcast_fusion.1
  54.8 0.3 fusion.43
  55.1 1.3 convolution_multiply_fusion.1
  56.4 3.0 %multiply_add_fusion = (f32[256,2048]{1,0:T(8,128)}, f32[256,2048]{1,0:T(8,128)}) fusion(f32[256,2048]{1,0:T(8,128)S(1)} %convolution_multiply_fusion.1, bf16[512,2048]{1,0:T(8,128)(2,1)S(1)} %get-tuple-element.65, bf16[512,2048]{1,0:T(8,128)(2,1)S(1)} %get-tuple-element.64, bf16[256,512]{1,0:T(8,128)(2,1)S(1)} %bitcast.84, bf16[256,512]{1,0:T(8,128)(2,1)S(1)} %bitcast.82), kind=kOutput, calls=%fused_computation.21 | convolution fusion | flops 1085276160 | bytes 11010048 | tf_op jit(solution)/shard_map/dot_general | solution.py:36
  59.4 1.8 %reduce_sum.27 = f32[64,2048]{1,0:T(8,128)S(1)} reduce(f32[4,64,2048]{2,1,0:T(8,128)} %bitcast.76, f32[]{:T(128)} %constant.126.clone.1), dimensions={0}, to_apply=%region_0.1 | reduce | flops 393216 | bytes 2621444 | tf_op jit(solution)/shard_map/reduce_sum | solution.py:120
  61.1 1.3 subtract_multiply_fusion
  62.4 2.9 %fusion.8 = (bf16[256,2048]{1,0:T(8,128)(2,1)S(1)}, bf16[256,2048]{1,0:T(8,128)(2,1)S(1)}) fusion(f32[256,2048]{1,0:T(8,128)} %get-tuple-element.69, f32[64,2048]{1,0:T(8,128)S(1)} %subtract_multiply_fusion, f32[256,2048]{1,0:T(8,128)} %copy-done), kind=kLoop, calls=%fused_computation.20 | loop fusion | flops 2097152 | bytes 6815744 | tf_op jit(solution)/shard_map/convert_element_type | solution.py:131
  65.4 1.3 fusion.107
  66.6 0.3 copy-done.5
  66.9 1.3 fusion.10
  68.2 0.3 convolution_bitcast_fusion.3
  68.5 0.3 convolution_bitcast_fusion.2
  68.8 0.9 add_reduce_fusion
  69.8 0.0 all-reduce.5.cloned.1.call-update
  69.8 32.6 %all-reduce.5.cloned.1.call-done = (bf16[48,512]{1,0:T(8,128)(2,1)}, bf16[48,512]{1,0:T(8,128)(2,1)}) async-done(((bf16[48,512]{1,0:T(8,128)(2,1)}, bf16[48,512]{1,0:T(8,128)(2,1)}), (bf16[48,512]{1,0:T(8,128)(2,1)}, bf16[48,512]{1,0:T(8,128)(2,1)})) %all-reduce.5.cloned.1.call-update) | async-done | bytes 98320 | tf_op jit(solution)/shard_map/psum | solution.py:145
  102.4 1.0 pad_maximum_fusion.14
  103.4 4.7 %collective-permute-start.3 = (bf16[1,2,48,512]{3,2,1,0:T(8,128)(2,1)S(1)}, bf16[1,2,48,512]{3,2,1,0:T(8,128)(2,1)S(1)}, u32[]{:S(2)}, u32[]{:S(2)}) collective-permute-start(bf16[1,2,48,512]{3,2,1,0:T(8,128)(2,1)S(1)} %pad_maximum_fusion.14), channel_id=1, source_target_pairs={{4,0},{8,4},{12,8},{5,1},{9,5},{13,9},{6,2},{10,6},{14,10},{7,3},{... | collective-permute-start | bytes 294920 | tf_op jit(solution)/shard_map/ppermute | solution.py:23
  108.1 3.2 %collective-permute-start.2 = (bf16[1,2,48,512]{3,2,1,0:T(8,128)(2,1)S(1)}, bf16[1,2,48,512]{3,2,1,0:T(8,128)(2,1)S(1)}, u32[]{:S(2)}, u32[]{:S(2)}) collective-permute-start(bf16[1,2,48,512]{3,2,1,0:T(8,128)(2,1)S(1)} %pad_maximum_fusion.14), channel_id=1, source_target_pairs={{0,4},{4,8},{8,12},{1,5},{5,9},{9,13},{2,6},{6,10},{10,14},{3,7},{... | collective-permute-start | bytes 294920 | tf_op jit(solution)/shard_map/ppermute | solution.py:20
  111.2 1.0 fusion.89
  112.3 1.1 fusion.87
  113.3 1.1 fusion.12
  114.4 1.1 fusion.11
  115.5 0.2 fusion.66
  115.7 0.2 fusion.67
  115.9 0.2 fusion.68
  116.0 0.2 fusion.69
  116.2 0.2 fusion.14
  116.4 0.2 fusion.13
  116.6 0.2 fusion.16
  116.8 0.2 fusion.15
  117.0 0.0 copy-start.6
  117.0 1.0 convolution_multiply_fusion.2
  118.1 0.2 fusion.41
  118.3 2.4 %collective-permute-start.4 = (bf16[1,2048]{1,0:T(2,128)(2,1)S(1)}, bf16[1,2048]{1,0:T(2,128)(2,1)S(1)}, u32[]{:S(2)}, u32[]{:S(2)}) collective-permute-start(bf16[1,2048]{1,0:T(2,128)(2,1)S(1)} %get-tuple-element.60), channel_id=1, source_target_pairs={{0,4},{4,8},{8,12},{1,5},{5,9},{9,13},{2,6},{6,10},{10,14},{3,7},{... | collective-permute-start | bytes 12296 | tf_op jit(solution)/shard_map/ppermute | solution.py:20
  120.7 1.9 %collective-permute-start.5 = (bf16[1,2048]{1,0:T(2,128)(2,1)S(1)}, bf16[1,2048]{1,0:T(2,128)(2,1)S(1)}, u32[]{:S(2)}, u32[]{:S(2)}) collective-permute-start(bf16[1,2048]{1,0:T(2,128)(2,1)S(1)} %get-tuple-element.61), channel_id=1, source_target_pairs={{4,0},{8,4},{12,8},{5,1},{9,5},{13,9},{6,2},{10,6},{14,10},{7,3},{... | collective-permute-start | bytes 12296 | tf_op jit(solution)/shard_map/ppermute | solution.py:23
  122.6 0.0 collective-permute-done.4
  122.6 3.0 %collective-permute-done.5 = bf16[1,2048]{1,0:T(2,128)(2,1)S(1)} collective-permute-done((bf16[1,2048]{1,0:T(2,128)(2,1)S(1)}, bf16[1,2048]{1,0:T(2,128)(2,1)S(1)}, u32[]{:S(2)}, u32[]{:S(2)}) %collective-permute-start.5) | collective-permute-done | bytes 4128 | tf_op jit(solution)/shard_map/ppermute | solution.py:23
  125.7 0.1 maximum_convert_fusion
  125.8 1.0 add_convert_fusion
  126.8 1.9 %collective-permute-start.6 = (bf16[1,2048]{1,0:T(2,128)(2,1)S(1)}, bf16[1,2048]{1,0:T(2,128)(2,1)S(1)}, u32[]{:S(2)}, u32[]{:S(2)}) collective-permute-start(bf16[1,2048]{1,0:T(2,128)(2,1)S(1)} %get-tuple-element.58), channel_id=1, source_target_pairs={{0,4},{4,8},{8,12},{1,5},{5,9},{9,13},{2,6},{6,10},{10,14},{3,7},{... | collective-permute-start | bytes 12296 | tf_op jit(solution)/shard_map/ppermute | solution.py:20
  128.7 2.4 %collective-permute-start.7 = (bf16[1,2048]{1,0:T(2,128)(2,1)S(1)}, bf16[1,2048]{1,0:T(2,128)(2,1)S(1)}, u32[]{:S(2)}, u32[]{:S(2)}) collective-permute-start(bf16[1,2048]{1,0:T(2,128)(2,1)S(1)} %get-tuple-element.59), channel_id=1, source_target_pairs={{4,0},{8,4},{12,8},{5,1},{9,5},{13,9},{6,2},{10,6},{14,10},{7,3},{... | collective-permute-start | bytes 12296 | tf_op jit(solution)/shard_map/ppermute | solution.py:23
  131.1 0.0 collective-permute-done.6
  131.1 2.6 %collective-permute-done.7 = bf16[1,2048]{1,0:T(2,128)(2,1)S(1)} collective-permute-done((bf16[1,2048]{1,0:T(2,128)(2,1)S(1)}, bf16[1,2048]{1,0:T(2,128)(2,1)S(1)}, u32[]{:S(2)}, u32[]{:S(2)}) %collective-permute-start.7) | collective-permute-done | bytes 4128 | tf_op jit(solution)/shard_map/ppermute | solution.py:23
  133.7 0.1 maximum_convert_fusion.1
  133.8 1.8 %multiply_add_fusion.1 = f32[64,2048]{1,0:T(8,128)} fusion(f32[66,2048]{1,0:T(8,128)S(1)} %maximum_convert_fusion.1), kind=kLoop, calls=%fused_computation.89 | loop fusion | flops 3670016 | bytes 2686976 | tf_op jit(solution)/shard_map/add | solution.py:77
  (21 shorter events, 0.1 us)
Async XLA Ops:
  6.5 95.9 %all-reduce.5.cloned.1.call-start = ((), (), s32[]{:S(2)}) async-start(), calls=%async_computation | async-start | bytes 196608 | tf_op jit(solution)/shard_map/psum | solution.py:145
  7.7 25.3 %copy-start.9 = (s32[512]{0:T(512)S(1)}, s32[512]{0:T(512)}, u32[]{:S(2)}) copy-start(s32[512]{0:T(512)} %param.21) | copy-start | bytes 6148
  7.7 43.2 %collective-permute-start.1 = (bf16[64,2048]{1,0:T(8,128)(2,1)S(1)}, bf16[64,2048]{1,0:T(8,128)(2,1)S(1)}, u32[]{:S(2)}, u32[]{:S(2)}) collective-permute-start(bf16[64,2048]{1,0:T(8,128)(2,1)S(1)} %tanh_convert_fusion), channel_id=1, source_target_pairs={{4,0},{8,4},{12,8},{5,1},{9,5},{13,9},{6,2},{10,6},{14,10},{7,3},{... | collective-permute-start | bytes 786440 | tf_op jit(solution)/shard_map/ppermute | solution.py:23
  9.6 41.3 %collective-permute-start = (bf16[64,2048]{1,0:T(8,128)(2,1)S(1)}, bf16[64,2048]{1,0:T(8,128)(2,1)S(1)}, u32[]{:S(2)}, u32[]{:S(2)}) collective-permute-start(bf16[64,2048]{1,0:T(8,128)(2,1)S(1)} %tanh_convert_fusion), channel_id=1, source_target_pairs={{0,4},{4,8},{8,12},{1,5},{5,9},{9,13},{2,6},{6,10},{10,14},{3,7},{... | collective-permute-start | bytes 786440 | tf_op jit(solution)/shard_map/ppermute | solution.py:20
  33.0 23.4 %copy-start.1 = (bf16[512,2048]{1,0:T(8,128)(2,1)}, bf16[512,2048]{1,0:T(8,128)(2,1)S(1)}, u32[]{:S(2)}) copy-start(bf16[512,2048]{1,0:T(8,128)(2,1)S(1)} %get-tuple-element.65) | copy-start | bytes 6291460
  33.0 23.4 %copy-start.4 = (bf16[512,2048]{1,0:T(8,128)(2,1)}, bf16[512,2048]{1,0:T(8,128)(2,1)S(1)}, u32[]{:S(2)}) copy-start(bf16[512,2048]{1,0:T(8,128)(2,1)S(1)} %get-tuple-element.64) | copy-start | bytes 6291460
  33.0 17.6 %copy-start.10 = (s32[48]{0:T(128)S(1)}, s32[48]{0:T(128)}, u32[]{:S(2)}) copy-start(s32[48]{0:T(128)} %param.20) | copy-start | bytes 580
  50.9 2.4 %copy-start.8 = (f32[48,512]{1,0:T(8,128)S(1)}, f32[48,512]{1,0:T(8,128)}, u32[]{:S(2)}) copy-start(f32[48,512]{1,0:T(8,128)} %param.19) | copy-start | bytes 294916
  52.5 1.2 copy-start.7
  56.4 3.0 %copy-start = (f32[256,2048]{1,0:T(8,128)}, f32[256,2048]{1,0:T(8,128)S(1)}, u32[]{:S(2)}) copy-start(f32[256,2048]{1,0:T(8,128)S(1)} %convolution_multiply_fusion.1) | copy-start | bytes 6291460
  62.4 2.9 %copy-start.2 = (bf16[512,2048]{1,0:T(8,128)(2,1)S(1)}, bf16[512,2048]{1,0:T(8,128)(2,1)}, u32[]{:S(2)}) copy-start(bf16[512,2048]{1,0:T(8,128)(2,1)} %copy-done.1) | copy-start | bytes 6291460
  65.4 1.6 %copy-start.5 = (bf16[512,2048]{1,0:T(8,128)(2,1)S(1)}, bf16[512,2048]{1,0:T(8,128)(2,1)}, u32[]{:S(2)}) copy-start(bf16[512,2048]{1,0:T(8,128)(2,1)} %copy-done.4) | copy-start | bytes 6291460
  102.4 14.6 %copy-start.3 = (bf16[512,2048]{1,0:T(8,128)(2,1)S(1)}, bf16[512,2048]{1,0:T(8,128)(2,1)}, u32[]{:S(2)}) copy-start(bf16[512,2048]{1,0:T(8,128)(2,1)} %copy-done.1) | copy-start | bytes 6291460
  103.4 12.5 %collective-permute-start.3 = (bf16[1,2,48,512]{3,2,1,0:T(8,128)(2,1)S(1)}, bf16[1,2,48,512]{3,2,1,0:T(8,128)(2,1)S(1)}, u32[]{:S(2)}, u32[]{:S(2)}) collective-permute-start(bf16[1,2,48,512]{3,2,1,0:T(8,128)(2,1)S(1)} %pad_maximum_fusion.14), channel_id=1, source_target_pairs={{4,0},{8,4},{12,8},{5,1},{9,5},{13,9},{6,2},{10,6},{14,10},{7,3},{... | collective-permute-start | bytes 294920 | tf_op jit(solution)/shard_map/ppermute | solution.py:23
  108.1 7.4 %collective-permute-start.2 = (bf16[1,2,48,512]{3,2,1,0:T(8,128)(2,1)S(1)}, bf16[1,2,48,512]{3,2,1,0:T(8,128)(2,1)S(1)}, u32[]{:S(2)}, u32[]{:S(2)}) collective-permute-start(bf16[1,2,48,512]{3,2,1,0:T(8,128)(2,1)S(1)} %pad_maximum_fusion.14), channel_id=1, source_target_pairs={{0,4},{4,8},{8,12},{1,5},{5,9},{9,13},{2,6},{6,10},{10,14},{3,7},{... | collective-permute-start | bytes 294920 | tf_op jit(solution)/shard_map/ppermute | solution.py:20
  117.0 1.1 copy-start.6
  118.3 4.3 %collective-permute-start.4 = (bf16[1,2048]{1,0:T(2,128)(2,1)S(1)}, bf16[1,2048]{1,0:T(2,128)(2,1)S(1)}, u32[]{:S(2)}, u32[]{:S(2)}) collective-permute-start(bf16[1,2048]{1,0:T(2,128)(2,1)S(1)} %get-tuple-element.60), channel_id=1, source_target_pairs={{0,4},{4,8},{8,12},{1,5},{5,9},{9,13},{2,6},{6,10},{10,14},{3,7},{... | collective-permute-start | bytes 12296 | tf_op jit(solution)/shard_map/ppermute | solution.py:20
  120.7 5.0 %collective-permute-start.5 = (bf16[1,2048]{1,0:T(2,128)(2,1)S(1)}, bf16[1,2048]{1,0:T(2,128)(2,1)S(1)}, u32[]{:S(2)}, u32[]{:S(2)}) collective-permute-start(bf16[1,2048]{1,0:T(2,128)(2,1)S(1)} %get-tuple-element.61), channel_id=1, source_target_pairs={{4,0},{8,4},{12,8},{5,1},{9,5},{13,9},{6,2},{10,6},{14,10},{7,3},{... | collective-permute-start | bytes 12296 | tf_op jit(solution)/shard_map/ppermute | solution.py:23
  126.8 4.3 %collective-permute-start.6 = (bf16[1,2048]{1,0:T(2,128)(2,1)S(1)}, bf16[1,2048]{1,0:T(2,128)(2,1)S(1)}, u32[]{:S(2)}, u32[]{:S(2)}) collective-permute-start(bf16[1,2048]{1,0:T(2,128)(2,1)S(1)} %get-tuple-element.58), channel_id=1, source_target_pairs={{0,4},{4,8},{8,12},{1,5},{5,9},{9,13},{2,6},{6,10},{10,14},{3,7},{... | collective-permute-start | bytes 12296 | tf_op jit(solution)/shard_map/ppermute | solution.py:20
  128.7 5.0 %collective-permute-start.7 = (bf16[1,2048]{1,0:T(2,128)(2,1)S(1)}, bf16[1,2048]{1,0:T(2,128)(2,1)S(1)}, u32[]{:S(2)}, u32[]{:S(2)}) collective-permute-start(bf16[1,2048]{1,0:T(2,128)(2,1)S(1)} %get-tuple-element.59), channel_id=1, source_target_pairs={{4,0},{8,4},{12,8},{5,1},{9,5},{13,9},{6,2},{10,6},{14,10},{7,3},{... | collective-permute-start | bytes 12296 | tf_op jit(solution)/shard_map/ppermute | solution.py:23
Sparse Core Ops, SparseCore 0:
  69.9 32.4 all-reduce.4
where the time goes:
time: 143 us; the launch traced here: 142 us
  other arithmetic  49 us (34%)
  waiting for transfers between devices  38.2 us (27%)
  starting transfers between devices  22.9 us (16%)
  matrix products  17.2 us (12%)
  between operations  14.6 us (10%)
    psum x1, waiting for transfers between devices, on_device(): lax.psum(y_im.astype(jnp.bfloat16), 'focus').astype(jnp.float32)  32.6 us
    convert_element_type x1, other arithmetic, tables(): jnp.sin(angles).astype(jnp.bfloat16)  18.9 us
    neg x1, other arithmetic, on_device(): forward = jnp.concatenate([col_cos, -col_sin], axis=0)  16.9 us
    ppermute x4, starting transfers between devices, padded_2(): lax.ppermute(lax.slice_in_dim(block, block.shape[dim] - width, None, axis...  12 us
    ppermute x4, starting transfers between devices, padded_2(): lax.ppermute(lax.slice_in_dim(block, 0, width, axis=dim), axis, backward)  10.9 us
    dot_general x5, matrix products, product(): return jnp.dot(lhs_mat, rhs_mat, preferred_element_type=jnp.float32)  6.07 us
    dot_general x12, matrix products, exact_t(): lax.dot_general(lhs_mat.astype(jnp.float32), rhs_mat, (((0,), (0,)), ((),...  5.65 us
    ppermute x4, waiting for transfers between devices, padded_2(): lax.ppermute(lax.slice_in_dim(block, 0, width, axis=dim), axis, backward)  5.61 us
  transfers between devices with their start and end apart: 9, of which 3 were waited for; matrix products, arithmetic and copies ran while one was open for 29% of the time, Pallas kernels for 0%

commit v1 on v0

--- a/solution.py
+++ b/solution.py
@@ -142,7 +142,7 @@
     y_im = jnp.sum(k_re * w_im - k_im * w_re, axis=0)
     y_re, y_im = (
         lax.psum(y_re.astype(jnp.bfloat16), "focus").astype(jnp.float32),
-        lax.psum(y_im.astype(jnp.bfloat16), "focus").astype(jnp.float32),
+        lax.all_gather(y_im.astype(jnp.bfloat16), "focus").sum(axis=0).astype(jnp.float32),
     )
     stacked = jnp.stack([y_re, y_im])[None]
     beside_all = padded_2(stacked.astype(jnp.bfloat16), (("strip", 0),), 1).astype(stacked.dtype)

time: 143 us -> 125 us (0.87)
  waiting for transfers between devices: 38.2 us -> 6.45 us
  blocking collectives: 0 us -> 27.4 us
  between operations: 14.6 us -> 1.22 us
  starting transfers between devices: 22.9 us -> 27.9 us
  matrix products: 17.2 us -> 14.1 us
  other arithmetic: 49 us -> 47.5 us
    psum x1 -> x0, waiting for transfers between devices: 32.6 us -> none  [on_device(): lax.psum(y_im.astype(jnp.bfloat16), 'focus').astype(jnp.float32)]
    psum x0 -> x1, blocking collectives: none -> 16.2 us  [on_device(): lax.psum(y_re.astype(jnp.bfloat16), 'focus').astype(jnp.float32)]
    all_gather x0 -> x1, blocking collectives: none -> 11.2 us  [on_device(): lax.all_gather(y_im.astype(jnp.bfloat16), 'focus').sum(axis=0)]
    dot_general x12, matrix products: 5.65 us -> 2.45 us  [exact_t(): lax.dot_general(lhs_mat.astype(jnp.float32), rhs_mat, (((0,), (0,)), ((),...]
    ppermute x4, starting transfers between devices: 10.9 us -> 14 us  [padded_2(): lax.ppermute(lax.slice_in_dim(block, 0, width, axis=dim), axis, backward)]
    ppermute x4, starting transfers between devices: 12 us -> 13.9 us  [padded_2(): lax.ppermute(lax.slice_in_dim(block, block.shape[dim] - width, None, axis...]
  transfers between devices with their start and end apart: 9 -> 8, of which waited for: 3 -> 3; matrix products, arithmetic and copies ran while one was open for 29% -> 30% of each run, Pallas kernels for 0% -> 0%
where the time goes in v1:
time: 125 us
  other arithmetic  47.5 us (38%)
  starting transfers between devices  27.9 us (22%)
  blocking collectives  27.4 us (22%)
  matrix products  14.1 us (11%)
  waiting for transfers between devices  6.45 us (5%)
    convert_element_type x1, other arithmetic, tables(): jnp.sin(angles).astype(jnp.bfloat16)  18.9 us
    neg x1, other arithmetic, on_device(): forward = jnp.concatenate([col_cos, -col_sin], axis=0)  16.9 us
    psum x1, blocking collectives, on_device(): lax.psum(y_re.astype(jnp.bfloat16), 'focus').astype(jnp.float32)  16.2 us
    ppermute x4, starting transfers between devices, padded_2(): lax.ppermute(lax.slice_in_dim(block, 0, width, axis=dim), axis, backward)  14 us
    ppermute x4, starting transfers between devices, padded_2(): lax.ppermute(lax.slice_in_dim(block, block.shape[dim] - width, None, axis...  13.9 us
    all_gather x1, blocking collectives, on_device(): lax.all_gather(y_im.astype(jnp.bfloat16), 'focus').sum(axis=0)  11.2 us
    dot_general x5, matrix products, product(): return jnp.dot(lhs_mat, rhs_mat, preferred_element_type=jnp.float32)  6.08 us
    ppermute x4, waiting for transfers between devices, padded_2(): lax.ppermute(lax.slice_in_dim(block, 0, width, axis=dim), axis, backward)  5.61 us
  transfers between devices with their start and end apart: 8, of which 3 were waited for; matrix products, arithmetic and copies ran while one was open for 30% of the time, Pallas kernels for 0%

profile of v1, /device:TPU:1, one launch (start us, length us, event | category | flops | bytes accessed | tf_op | source)
XLA Modules:
  0.0 124.9 jit_solution(2084387285716563858)
XLA Ops:
  0.0 1.1 tanh_convert_fusion
  1.1 0.0 copy-start.9
  1.1 1.9 %collective-permute-start.1 = (bf16[64,2048]{1,0:T(8,128)(2,1)S(1)}, bf16[64,2048]{1,0:T(8,128)(2,1)S(1)}, u32[]{:S(2)}, u32[]{:S(2)}) collective-permute-start(bf16[64,2048]{1,0:T(8,128)(2,1)S(1)} %tanh_convert_fusion), channel_id=1, source_target_pairs={{4,0},{8,4},{12,8},{5,1},{9,5},{13,9},{6,2},{10,6},{14,10},{7,3},{... | collective-permute-start | bytes 786440 | tf_op jit(solution)/shard_map/ppermute | solution.py:23
  3.1 4.5 %collective-permute-start = (bf16[64,2048]{1,0:T(8,128)(2,1)S(1)}, bf16[64,2048]{1,0:T(8,128)(2,1)S(1)}, u32[]{:S(2)}, u32[]{:S(2)}) collective-permute-start(bf16[64,2048]{1,0:T(8,128)(2,1)S(1)} %tanh_convert_fusion), channel_id=1, source_target_pairs={{0,4},{4,8},{8,12},{1,5},{5,9},{9,13},{2,6},{6,10},{10,14},{3,7},{... | collective-permute-start | bytes 786440 | tf_op jit(solution)/shard_map/ppermute | solution.py:20
  7.6 18.9 %sine_convert_fusion = (bf16[512,2048]{1,0:T(8,128)(2,1)S(1)}, bf16[512,2048]{1,0:T(8,128)(2,1)S(1)}) fusion(s32[512]{0:T(512)} %param.21), kind=kLoop, calls=%fused_computation.8 | loop fusion | flops 16777216 | bytes 4196352 | tf_op jit(solution)/shard_map/convert_element_type | solution.py:32
  26.5 0.0 copy-start.10
  26.5 16.9 %fusion.22 = bf16[512,2048]{1,0:T(8,128)(2,1)S(1)} fusion(s32[512]{0:T(512)S(1)} %copy-done.9), kind=kLoop, calls=%fused_computation.50 | loop fusion | flops 18874368 | bytes 2099200 | tf_op jit(solution)/shard_map/neg | solution.py:88
  44.1 0.3 cosine_convert_fusion.1
  44.4 0.0 collective-permute-done.1
  44.4 0.0 copy-start.8
  44.4 1.6 %convolution_convert_fusion = bf16[192,1024]{1,0:T(8,128)(2,1)S(1)} fusion(bf16[64,2048]{1,0:T(8,128)(2,1)S(1)} %collective-permute-done.1, bf16[64,2048]{1,0:T(8,128)(2,1)S(1)} %tanh_convert_fusion, bf16[64,2048]{1,0:T(8,128)(2,1)S(1)} %collective-permute-done, bf16[512,2048]{1,0:T(8,128)(2,1)S(1)} %fusion.22, bf16[512,2048]{1,0:T(8,128)(2,1)S(1)} %get-tuple-element.63), kind=kOutput, calls=%fused_computation.28 | convolution fusion | flops 816250880 | bytes 5373952 | tf_op jit(solution)/shard_map/dot_general | solution.py:40
  45.9 0.0 copy-start.7
  46.0 0.4 fusion.93
  46.4 0.4 fusion.92
  46.8 0.4 fusion.60
  47.2 0.2 subtract_convert_fusion
  47.4 0.1 add_convert_fusion.1
  47.5 0.4 convolution_bitcast_fusion
  47.9 0.4 convolution_bitcast_fusion.1
  48.3 0.3 fusion.43
  48.6 1.3 %convolution_multiply_fusion.1 = f32[256,2048]{1,0:T(8,128)S(1)} fusion(bf16[256,512]{1,0:T(8,128)(2,1)S(1)} %bitcast.85, bf16[256,512]{1,0:T(8,128)(2,1)S(1)} %bitcast.83, bf16[512,2048]{1,0:T(8,128)(2,1)S(1)} %fusion.22, bf16[512,2048]{1,0:T(8,128)(2,1)S(1)} %get-tuple-element.63), kind=kOutput, calls=%fused_computation.16 | convolution fusion | flops 1083703296 | bytes 6815744 | tf_op jit(solution)/shard_map/dot_general | solution.py:36
  49.9 3.0 %multiply_add_fusion = (f32[256,2048]{1,0:T(8,128)}, f32[256,2048]{1,0:T(8,128)}) fusion(f32[256,2048]{1,0:T(8,128)S(1)} %convolution_multiply_fusion.1, bf16[512,2048]{1,0:T(8,128)(2,1)S(1)} %get-tuple-element.63, bf16[512,2048]{1,0:T(8,128)(2,1)S(1)} %get-tuple-element.62, bf16[256,512]{1,0:T(8,128)(2,1)S(1)} %bitcast.86, bf16[256,512]{1,0:T(8,128)(2,1)S(1)} %bitcast.84), kind=kOutput, calls=%fused_computation.21 | convolution fusion | flops 1085276160 | bytes 11010048 | tf_op jit(solution)/shard_map/dot_general | solution.py:36
  52.8 1.8 %reduce_sum.39 = f32[64,2048]{1,0:T(8,128)S(1)} reduce(f32[4,64,2048]{2,1,0:T(8,128)} %bitcast.77, f32[]{:T(128)} %constant.127.clone.1), dimensions={0}, to_apply=%region_0.1 | reduce | flops 393216 | bytes 2621444 | tf_op jit(solution)/shard_map/reduce_sum | solution.py:120
  54.6 1.3 %subtract_multiply_fusion = f32[64,2048]{1,0:T(8,128)S(1)} fusion(s32[64,2048]{1,0:T(8,128)} %param.16, f32[64,2048]{1,0:T(8,128)S(1)} %reduce_sum.39), kind=kLoop, calls=%fused_computation.91 | loop fusion | flops 1572864 | bytes 1572864 | tf_op jit(solution)/shard_map/mul | solution.py:123
  55.9 2.9 %fusion.8 = (bf16[256,2048]{1,0:T(8,128)(2,1)S(1)}, bf16[256,2048]{1,0:T(8,128)(2,1)S(1)}) fusion(f32[256,2048]{1,0:T(8,128)} %get-tuple-element.67, f32[64,2048]{1,0:T(8,128)S(1)} %subtract_multiply_fusion, f32[256,2048]{1,0:T(8,128)} %copy-done), kind=kLoop, calls=%fused_computation.20 | loop fusion | flops 2097152 | bytes 6815744 | tf_op jit(solution)/shard_map/convert_element_type | solution.py:131
  58.8 1.3 %fusion.107 = f32[256,1024]{1,0:T(8,128)S(1)} fusion(bf16[256,2048]{1,0:T(8,128)(2,1)S(1)} %get-tuple-element.53, bf16[512,2048]{1,0:T(8,128)(2,1)S(1)} %fusion.22, bf16[512,2048]{1,0:T(8,128)(2,1)S(1)} %copy-done.2), kind=kOutput, calls=%fused_computation.182 | convolution fusion | flops 1082130432 | bytes 6291456 | tf_op jit(solution)/shard_map/dot_general | solution.py:40
  60.1 0.3 copy-done.5
  60.4 1.3 %fusion.10 = bf16[256,1024]{1,0:T(8,128)(2,1)S(1)} fusion(f32[256,1024]{1,0:T(8,128)S(1)} %fusion.107, bf16[256,2048]{1,0:T(8,128)(2,1)S(1)} %get-tuple-element.52, bf16[512,2048]{1,0:T(8,128)(2,1)S(1)} %copy-done.2, bf16[512,2048]{1,0:T(8,128)(2,1)S(1)} %copy-done.5), kind=kOutput, calls=%fused_computation.25 | convolution fusion | flops 1082654720 | bytes 6815744 | tf_op jit(solution)/shard_map/dot_general | solution.py:40
  61.7 0.3 convolution_bitcast_fusion.3
  62.0 0.3 convolution_bitcast_fusion.2
  62.3 0.3 add_reduce_fusion
  62.6 16.2 %psum.7 = bf16[48,512]{1,0:T(8,128)(2,1)S(1)} all-reduce(bf16[48,512]{1,0:T(8,128)(2,1)S(1)} %get-tuple-element.45), channel_id=1, replica_groups=mesh['tile'=2,'strip'=4,'focus'=4] {'focus'}, use_global_device_ids=true, to_apply=%region_2.3 | all-reduce | flops 24576 | bytes 98304 | tf_op jit(solution)/shard_map/psum | solution.py:144
  78.8 0.2 fusion.87
  79.1 11.2 %all-gather = bf16[192,512]{1,0:T(8,128)(2,1)S(1)} all-gather(bf16[48,512]{1,0:T(8,128)(2,1)S(1)} %get-tuple-element.46), channel_id=2, replica_groups=mesh['tile'=2,'strip'=4,'focus'=4] {'focus'}, dimensions={0}, use_global_device_ids=true | all-gather | bytes 245760 | tf_op jit(solution)/shard_map/all_gather | solution.py:145
  90.3 7.8 %collective-permute-start.3 = (bf16[1,2,48,512]{3,2,1,0:T(8,128)(2,1)S(1)}, bf16[1,2,48,512]{3,2,1,0:T(8,128)(2,1)S(1)}, u32[]{:S(2)}, u32[]{:S(2)}) collective-permute-start(bf16[1,2,48,512]{3,2,1,0:T(8,128)(2,1)S(1)} %pad_maximum_fusion.14), channel_id=1, source_target_pairs={{4,0},{8,4},{12,8},{5,1},{9,5},{13,9},{6,2},{10,6},{14,10},{7,3},{... | collective-permute-start | bytes 294920 | tf_op jit(solution)/shard_map/ppermute | solution.py:23
  98.1 3.1 %collective-permute-start.2 = (bf16[1,2,48,512]{3,2,1,0:T(8,128)(2,1)S(1)}, bf16[1,2,48,512]{3,2,1,0:T(8,128)(2,1)S(1)}, u32[]{:S(2)}, u32[]{:S(2)}) collective-permute-start(bf16[1,2,48,512]{3,2,1,0:T(8,128)(2,1)S(1)} %pad_maximum_fusion.14), channel_id=1, source_target_pairs={{0,4},{4,8},{8,12},{1,5},{5,9},{9,13},{2,6},{6,10},{10,14},{3,7},{... | collective-permute-start | bytes 294920 | tf_op jit(solution)/shard_map/ppermute | solution.py:20
  101.3 0.2 fusion.89
  101.5 0.3 fusion.11
  101.8 0.3 fusion.12
  102.0 0.8 collective-permute-done.2
  102.9 0.2 fusion.66
  103.1 0.2 fusion.67
  103.2 0.0 collective-permute-done.3
  103.3 0.2 fusion.68
  103.4 0.2 fusion.69
  103.6 0.2 fusion.14
  103.8 0.2 fusion.13
  104.0 0.2 fusion.16
  104.2 0.2 fusion.15
  104.4 0.0 copy-start.6
  104.4 1.0 convolution_multiply_fusion.2
  105.5 0.2 fusion.41
  105.7 4.3 %collective-permute-start.4 = (bf16[1,2048]{1,0:T(2,128)(2,1)S(1)}, bf16[1,2048]{1,0:T(2,128)(2,1)S(1)}, u32[]{:S(2)}, u32[]{:S(2)}) collective-permute-start(bf16[1,2048]{1,0:T(2,128)(2,1)S(1)} %get-tuple-element.58), channel_id=1, source_target_pairs={{0,4},{4,8},{8,12},{1,5},{5,9},{9,13},{2,6},{6,10},{10,14},{3,7},{... | collective-permute-start | bytes 12296 | tf_op jit(solution)/shard_map/ppermute | solution.py:20
  110.0 1.9 %collective-permute-start.5 = (bf16[1,2048]{1,0:T(2,128)(2,1)S(1)}, bf16[1,2048]{1,0:T(2,128)(2,1)S(1)}, u32[]{:S(2)}, u32[]{:S(2)}) collective-permute-start(bf16[1,2048]{1,0:T(2,128)(2,1)S(1)} %get-tuple-element.59), channel_id=1, source_target_pairs={{4,0},{8,4},{12,8},{5,1},{9,5},{13,9},{6,2},{10,6},{14,10},{7,3},{... | collective-permute-start | bytes 12296 | tf_op jit(solution)/shard_map/ppermute | solution.py:23
  111.9 0.0 collective-permute-done.4
  112.0 3.0 %collective-permute-done.5 = bf16[1,2048]{1,0:T(2,128)(2,1)S(1)} collective-permute-done((bf16[1,2048]{1,0:T(2,128)(2,1)S(1)}, bf16[1,2048]{1,0:T(2,128)(2,1)S(1)}, u32[]{:S(2)}, u32[]{:S(2)}) %collective-permute-start.5) | collective-permute-done | bytes 4128 | tf_op jit(solution)/shard_map/ppermute | solution.py:23
  115.0 0.1 maximum_convert_fusion
  115.1 1.0 add_convert_fusion
  116.1 1.9 %collective-permute-start.6 = (bf16[1,2048]{1,0:T(2,128)(2,1)S(1)}, bf16[1,2048]{1,0:T(2,128)(2,1)S(1)}, u32[]{:S(2)}, u32[]{:S(2)}) collective-permute-start(bf16[1,2048]{1,0:T(2,128)(2,1)S(1)} %get-tuple-element.56), channel_id=1, source_target_pairs={{0,4},{4,8},{8,12},{1,5},{5,9},{9,13},{2,6},{6,10},{10,14},{3,7},{... | collective-permute-start | bytes 12296 | tf_op jit(solution)/shard_map/ppermute | solution.py:20
  118.0 2.4 %collective-permute-start.7 = (bf16[1,2048]{1,0:T(2,128)(2,1)S(1)}, bf16[1,2048]{1,0:T(2,128)(2,1)S(1)}, u32[]{:S(2)}, u32[]{:S(2)}) collective-permute-start(bf16[1,2048]{1,0:T(2,128)(2,1)S(1)} %get-tuple-element.57), channel_id=1, source_target_pairs={{4,0},{8,4},{12,8},{5,1},{9,5},{13,9},{6,2},{10,6},{14,10},{7,3},{... | collective-permute-start | bytes 12296 | tf_op jit(solution)/shard_map/ppermute | solution.py:23
  120.4 0.0 collective-permute-done.6
  120.4 2.6 %collective-permute-done.7 = bf16[1,2048]{1,0:T(2,128)(2,1)S(1)} collective-permute-done((bf16[1,2048]{1,0:T(2,128)(2,1)S(1)}, bf16[1,2048]{1,0:T(2,128)(2,1)S(1)}, u32[]{:S(2)}, u32[]{:S(2)}) %collective-permute-start.7) | collective-permute-done | bytes 4128 | tf_op jit(solution)/shard_map/ppermute | solution.py:23
  123.0 0.1 maximum_convert_fusion.1
  123.1 1.8 %multiply_add_fusion.1 = f32[64,2048]{1,0:T(8,128)} fusion(f32[66,2048]{1,0:T(8,128)S(1)} %maximum_convert_fusion.1), kind=kLoop, calls=%fused_computation.89 | loop fusion | flops 3670016 | bytes 2686976 | tf_op jit(solution)/shard_map/add | solution.py:77
  (21 shorter events, 0.1 us)
Async XLA Ops:
  1.1 25.3 %copy-start.9 = (s32[512]{0:T(512)S(1)}, s32[512]{0:T(512)}, u32[]{:S(2)}) copy-start(s32[512]{0:T(512)} %param.21) | copy-start | bytes 6148
  1.1 43.2 %collective-permute-start.1 = (bf16[64,2048]{1,0:T(8,128)(2,1)S(1)}, bf16[64,2048]{1,0:T(8,128)(2,1)S(1)}, u32[]{:S(2)}, u32[]{:S(2)}) collective-permute-start(bf16[64,2048]{1,0:T(8,128)(2,1)S(1)} %tanh_convert_fusion), channel_id=1, source_target_pairs={{4,0},{8,4},{12,8},{5,1},{9,5},{13,9},{6,2},{10,6},{14,10},{7,3},{... | collective-permute-start | bytes 786440 | tf_op jit(solution)/shard_map/ppermute | solution.py:23
  3.1 41.3 %collective-permute-start = (bf16[64,2048]{1,0:T(8,128)(2,1)S(1)}, bf16[64,2048]{1,0:T(8,128)(2,1)S(1)}, u32[]{:S(2)}, u32[]{:S(2)}) collective-permute-start(bf16[64,2048]{1,0:T(8,128)(2,1)S(1)} %tanh_convert_fusion), channel_id=1, source_target_pairs={{0,4},{4,8},{8,12},{1,5},{5,9},{9,13},{2,6},{6,10},{10,14},{3,7},{... | collective-permute-start | bytes 786440 | tf_op jit(solution)/shard_map/ppermute | solution.py:20
  26.4 23.4 %copy-start.1 = (bf16[512,2048]{1,0:T(8,128)(2,1)}, bf16[512,2048]{1,0:T(8,128)(2,1)S(1)}, u32[]{:S(2)}) copy-start(bf16[512,2048]{1,0:T(8,128)(2,1)S(1)} %get-tuple-element.63) | copy-start | bytes 6291460
  26.4 23.4 %copy-start.4 = (bf16[512,2048]{1,0:T(8,128)(2,1)}, bf16[512,2048]{1,0:T(8,128)(2,1)S(1)}, u32[]{:S(2)}) copy-start(bf16[512,2048]{1,0:T(8,128)(2,1)S(1)} %get-tuple-element.62) | copy-start | bytes 6291460
  26.5 17.6 %copy-start.10 = (s32[48]{0:T(128)S(1)}, s32[48]{0:T(128)}, u32[]{:S(2)}) copy-start(s32[48]{0:T(128)} %param.20) | copy-start | bytes 580
  44.4 2.4 %copy-start.8 = (f32[48,512]{1,0:T(8,128)S(1)}, f32[48,512]{1,0:T(8,128)}, u32[]{:S(2)}) copy-start(f32[48,512]{1,0:T(8,128)} %param.19) | copy-start | bytes 294916
  45.9 1.2 copy-start.7
  49.8 3.0 %copy-start = (f32[256,2048]{1,0:T(8,128)}, f32[256,2048]{1,0:T(8,128)S(1)}, u32[]{:S(2)}) copy-start(f32[256,2048]{1,0:T(8,128)S(1)} %convolution_multiply_fusion.1) | copy-start | bytes 6291460
  55.9 2.9 %copy-start.2 = (bf16[512,2048]{1,0:T(8,128)(2,1)S(1)}, bf16[512,2048]{1,0:T(8,128)(2,1)}, u32[]{:S(2)}) copy-start(bf16[512,2048]{1,0:T(8,128)(2,1)} %copy-done.1) | copy-start | bytes 6291460
  58.8 1.6 %copy-start.5 = (bf16[512,2048]{1,0:T(8,128)(2,1)S(1)}, bf16[512,2048]{1,0:T(8,128)(2,1)}, u32[]{:S(2)}) copy-start(bf16[512,2048]{1,0:T(8,128)(2,1)} %copy-done.4) | copy-start | bytes 6291460
  90.3 14.1 %copy-start.3 = (bf16[512,2048]{1,0:T(8,128)(2,1)S(1)}, bf16[512,2048]{1,0:T(8,128)(2,1)}, u32[]{:S(2)}) copy-start(bf16[512,2048]{1,0:T(8,128)(2,1)} %copy-done.1) | copy-start | bytes 6291460
  90.3 12.9 %collective-permute-start.3 = (bf16[1,2,48,512]{3,2,1,0:T(8,128)(2,1)S(1)}, bf16[1,2,48,512]{3,2,1,0:T(8,128)(2,1)S(1)}, u32[]{:S(2)}, u32[]{:S(2)}) collective-permute-start(bf16[1,2,48,512]{3,2,1,0:T(8,128)(2,1)S(1)} %pad_maximum_fusion.14), channel_id=1, source_target_pairs={{4,0},{8,4},{12,8},{5,1},{9,5},{13,9},{6,2},{10,6},{14,10},{7,3},{... | collective-permute-start | bytes 294920 | tf_op jit(solution)/shard_map/ppermute | solution.py:23
  98.1 4.7 %collective-permute-start.2 = (bf16[1,2,48,512]{3,2,1,0:T(8,128)(2,1)S(1)}, bf16[1,2,48,512]{3,2,1,0:T(8,128)(2,1)S(1)}, u32[]{:S(2)}, u32[]{:S(2)}) collective-permute-start(bf16[1,2,48,512]{3,2,1,0:T(8,128)(2,1)S(1)} %pad_maximum_fusion.14), channel_id=1, source_target_pairs={{0,4},{4,8},{8,12},{1,5},{5,9},{9,13},{2,6},{6,10},{10,14},{3,7},{... | collective-permute-start | bytes 294920 | tf_op jit(solution)/shard_map/ppermute | solution.py:20
  104.4 1.1 copy-start.6
  105.7 6.2 %collective-permute-start.4 = (bf16[1,2048]{1,0:T(2,128)(2,1)S(1)}, bf16[1,2048]{1,0:T(2,128)(2,1)S(1)}, u32[]{:S(2)}, u32[]{:S(2)}) collective-permute-start(bf16[1,2048]{1,0:T(2,128)(2,1)S(1)} %get-tuple-element.58), channel_id=1, source_target_pairs={{0,4},{4,8},{8,12},{1,5},{5,9},{9,13},{2,6},{6,10},{10,14},{3,7},{... | collective-permute-start | bytes 12296 | tf_op jit(solution)/shard_map/ppermute | solution.py:20
  110.0 5.0 %collective-permute-start.5 = (bf16[1,2048]{1,0:T(2,128)(2,1)S(1)}, bf16[1,2048]{1,0:T(2,128)(2,1)S(1)}, u32[]{:S(2)}, u32[]{:S(2)}) collective-permute-start(bf16[1,2048]{1,0:T(2,128)(2,1)S(1)} %get-tuple-element.59), channel_id=1, source_target_pairs={{4,0},{8,4},{12,8},{5,1},{9,5},{13,9},{6,2},{10,6},{14,10},{7,3},{... | collective-permute-start | bytes 12296 | tf_op jit(solution)/shard_map/ppermute | solution.py:23
  116.1 4.3 %collective-permute-start.6 = (bf16[1,2048]{1,0:T(2,128)(2,1)S(1)}, bf16[1,2048]{1,0:T(2,128)(2,1)S(1)}, u32[]{:S(2)}, u32[]{:S(2)}) collective-permute-start(bf16[1,2048]{1,0:T(2,128)(2,1)S(1)} %get-tuple-element.56), channel_id=1, source_target_pairs={{0,4},{4,8},{8,12},{1,5},{5,9},{9,13},{2,6},{6,10},{10,14},{3,7},{... | collective-permute-start | bytes 12296 | tf_op jit(solution)/shard_map/ppermute | solution.py:20
  118.0 5.0 %collective-permute-start.7 = (bf16[1,2048]{1,0:T(2,128)(2,1)S(1)}, bf16[1,2048]{1,0:T(2,128)(2,1)S(1)}, u32[]{:S(2)}, u32[]{:S(2)}) collective-permute-start(bf16[1,2048]{1,0:T(2,128)(2,1)S(1)} %get-tuple-element.57), channel_id=1, source_target_pairs={{4,0},{8,4},{12,8},{5,1},{9,5},{13,9},{6,2},{10,6},{14,10},{7,3},{... | collective-permute-start | bytes 12296 | tf_op jit(solution)/shard_map/ppermute | solution.py:23
